TPU v7x, 128 devices: a whole 4x4x4 slice. The times are simulated.
128 devices in a mesh: row: 4 (over x), col: 16 (over z, y), depth: 2 (over core).
Axes of the slice: x: 4, y: 4, z: 4, core: 2. Of those that a mesh axis runs over, the one named last changes fastest.
Arguments:
- tokens: bfloat16 [2048, 8192], P('depth', 'col'), may hold values from -6 to 6
- weight: bfloat16 [8192, 14336], P('col', ('row', 'depth')), may hold values from -0.0625 to 0.0625
- block_mask: int32 [64, 112], replicated, may hold values 0 or 1
- cotangent: bfloat16 [2048, 14336], P('depth', 'row'), may hold values from -6 to 6
- example_ids: int32 [2048], replicated, may hold values from 0 to 3, as said below
Outputs:
- outputs: bfloat16 [2048, 14336], P('depth', 'row')
- grad_in: bfloat16 [2048, 8192], P('depth', 'col')
- grad_weight: bfloat16 [8192, 14336], P('col', ('row', 'depth'))
Inputs may be any that keep to these rules, and one draw needn't show every extreme that they name: `example_ids`: in the b-th aligned block of 1024 tokens (b from 0), the ids are 2 b for a first run of tokens and 2 b + 1 for the rest; each example has at least 128 tokens, and in every draw some example has exactly 896.
All inputs are finite; a program needn't handle non-finite values.
Results may differ from a plain program's by a relative error of at most 0.0052.
Values may be sent and summed in bfloat16 or wider, within the bound.
A program may use at most 128 MiB of HBM per device.

v0:
```python
import math

import jax
import jax.numpy as jnp
from jax import lax
from jax.sharding import PartitionSpec as P

D = 8192
FW = 14336
BLOCK = 128
TOK_DEV = 1024
EX_DEV = 2


def total_squares(partial_squares):
    return lax.psum(partial_squares, ("row", "col"))


def shards(tokens, weight, block_mask, cotangent, example_ids):
    tok_rows = tokens.shape[0]
    width_here = tokens.shape[1]
    hidden_here = cotangent.shape[1]
    col_at = lax.axis_index("col")
    row_at = lax.axis_index("row")
    depth_at = lax.axis_index("depth")
    tile_mask = lax.dynamic_slice(
        block_mask,
        (col_at * (width_here // BLOCK), row_at * (hidden_here // BLOCK)),
        (width_here // BLOCK, hidden_here // BLOCK),
    )
    keep = jnp.repeat(jnp.repeat(tile_mask > 0, BLOCK, axis=0), BLOCK, axis=1)
    zero_half = jnp.zeros((), jnp.bfloat16)
    ids_here = lax.dynamic_slice_in_dim(example_ids, depth_at * tok_rows, tok_rows)
    per_grads = []
    squares = []
    for slot in range(EX_DEV):
        chosen = ids_here == depth_at * EX_DEV + slot
        picked = jnp.where(chosen[:, None], cotangent, zero_half)
        product = lax.dot_general(
            tokens, picked, (((0,), (0,)), ((), ())), preferred_element_type=jnp.float32
        )
        product = jnp.where(keep, product, jnp.float32(0.0))
        per_grads.append(product)
        squares.append(jnp.sum(product * product))
    partial_squares = jnp.stack(squares)
    kept = keep
    out_part = jnp.dot(
        tokens,
        jnp.where(kept, lax.all_gather(weight, "depth", axis=1, tiled=True), zero_half),
        preferred_element_type=jnp.float32,
    )
    kept = keep
    masked_piece = jnp.where(kept, lax.all_gather(weight, "depth", axis=1, tiled=True), zero_half)
    back_part = lax.dot_general(
        cotangent, masked_piece, (((1,), (1,)), ((), ())), preferred_element_type=jnp.float32
    )
    out_sum = lax.psum(out_part, "col")
    back_sum = lax.psum(back_part, "row")
    all_squares = total_squares(partial_squares)
    out_final = out_sum.astype(jnp.bfloat16)
    back_final = back_sum.astype(jnp.bfloat16)
    bound = jnp.float32(0.5 * math.sqrt(D * FW * TOK_DEV))
    norms = jnp.sqrt(all_squares)
    factors = bound / jnp.maximum(norms, bound)
    examples_all = EX_DEV * lax.axis_size("depth")
    combined = jnp.zeros((width_here, hidden_here), jnp.float32)
    for slot in range(EX_DEV):
        combined = combined + factors[slot] * per_grads[slot]
    combined = combined / examples_all
    grad_sum = lax.psum_scatter(
        combined.astype(jnp.bfloat16), "depth", scatter_dimension=1, tiled=True
    )
    return (out_final, back_final, grad_sum)


def solution(mesh):
    placed = (P("depth", "col"), P("col", ("row", "depth")), P(), P("depth", "row"), P())
    return jax.shard_map(
        shards,
        mesh=mesh,
        in_specs=placed,
        out_specs=(P("depth", "row"), P("depth", "col"), P("col", ("row", "depth"))),
        check_vma=False,
    )
```

profile of v0, /device:TPU:0, one launch (start us, length us, event | category | flops | bytes accessed | tf_op | source)
XLA Modules:
  0.0 582.8 jit_solution(15162042323849801208)
XLA Ops:
  7.2 0.0 all-gather.2.cloned.1.call-start
  7.2 3.9 copy.9
  11.1 0.0 all-gather.2.cloned.1.call-update
  11.2 0.0 reduce-scatter.2.cloned.1.call-start
  11.2 0.8 dynamic-slice_compare_fusion.2
  12.0 0.1 copy.8
  12.1 0.1 broadcast_bitcast_fusion
  12.3 0.7 dynamic-slice_compare_fusion
  13.0 6.5 %fusion = f32[3584,512]{1,0:T(8,128)S(1)} fusion(bf16[1024,512]{1,0:T(8,128)(2,1)S(1)} %copy-done, bf16[1024,3584]{1,0:T(8,128)(2,1)} %param.8, pred[1024]{0:T(1024)(128)(4,1)S(1)} %get-tuple-element.8), kind=kOutput, calls=%fused_computation.6 | convolution fusion | flops 3761766400 | bytes 15729664 | tf_op jit(solution)/shard_map/dot_general | solution.py:39
  19.5 14.7 %multiply_reduce_fusion.1 = (f32[]{:T(128)}, f32[]{:T(128)}, f32[3584,512]{1,0:T(8,128)}) fusion(pred[512,28]{0,1:T(8,128)(4,1)S(1)} %bitcast.44, f32[3584,512]{1,0:T(8,128)S(1)} %fusion, bf16[1024,512]{1,0:T(8,128)(2,1)S(1)} %copy-done, bf16[1024,3584]{1,0:T(8,128)(2,1)} %param.8, pred[1024]{0:T(1024)(128)(4,1)S(1)} %get-tuple-element.9), kind=kOutput, calls=%fused_computation.8 | convolution fusion | flops 3772776448 | bytes 23084040 | tf_op jit(solution)/shard_map/dot_general | solution.py:39
  34.2 1.3 pad_maximum_fusion
  35.5 180.6 %psum.23 = f32[2]{0:T(128)S(1)} all-reduce(f32[2]{0:T(128)S(1)} %pad_maximum_fusion), channel_id=1, replica_groups=mesh['row'=4,'col'=16,'depth'=2] {'row','col'}, use_global_device_ids=true, to_apply=%region_4.5 | all-reduce | flops 2 | bytes 16 | tf_op jit(solution)/shard_map/psum | solution.py:16
  216.1 0.6 fusion.10
  216.7 9.2 %multiply_convert_fusion = bf16[512,3584]{0,1:T(8,128)(2,1)} fusion(f32[3584,512]{1,0:T(8,128)} %get-tuple-element.12, f32[3584,512]{1,0:T(8,128)} %copy-done.1, f32[]{:T(128)} %bitcast.8, f32[]{:T(128)} %bitcast.7, pred[512,28]{0,1:T(8,128)(4,1)S(1)} %bitcast.45), kind=kLoop, calls=%fused_computation.4 | loop fusion | flops 12845056 | bytes 18364424 | tf_op jit(solution)/shard_map/convert_element_type | solution.py:71
  225.9 0.0 reduce-scatter.2.cloned.1.call-update
  225.9 0.0 all-gather.2.cloned.1.call-done
  226.0 2.3 bitcast_select_fusion.2
  228.3 7.8 %convolution_bitcast_fusion.1 = f32[1024,512]{0,1:T(8,128)} fusion(bf16[512,3584]{0,1:T(8,128)(2,1)S(1)} %bitcast_select_fusion.2, bf16[1024,3584]{1,0:T(8,128)(2,1)} %param.8), kind=kOutput, calls=%fused_computation.15 | convolution fusion | flops 3758096384 | bytes 13107200 | tf_op jit(solution)/shard_map/dot_general | solution.py:54
  236.1 7.3 %convolution_bitcast_fusion = f32[1024,3584]{0,1:T(8,128)} fusion(bf16[512,3584]{0,1:T(8,128)(2,1)S(1)} %bitcast_select_fusion.2, bf16[1024,512]{1,0:T(8,128)(2,1)S(1)} %copy-done), kind=kOutput, calls=%fused_computation.3 | convolution fusion | flops 3758096384 | bytes 19398656 | tf_op jit(solution)/shard_map/dot_general | solution.py:47
  243.4 31.6 %all-reduce.2 = bf16[1024,512]{0,1:T(8,128)(2,1)S(1)} all-reduce(f32[1024,512]{0,1:T(8,128)} %convolution_bitcast_fusion.1), channel_id=1, replica_groups=mesh['row'=4,'col'=16,'depth'=2] {'row'}, use_global_device_ids=true, to_apply=%region_1.2 | all-reduce | flops 524288 | bytes 3145728 | tf_op jit(solution)/shard_map/psum | solution.py:58
  275.0 1.3 copy.11
  276.4 285.8 %all-reduce.3 = bf16[1024,3584]{0,1:T(8,128)(2,1)} all-reduce(f32[1024,3584]{0,1:T(8,128)} %convolution_bitcast_fusion), channel_id=1, replica_groups=mesh['row'=4,'col'=16,'depth'=2] {'col'}, use_global_device_ids=true, to_apply=%region_0.1 | all-reduce | flops 3670016 | bytes 22020096 | tf_op jit(solution)/shard_map/psum | solution.py:57
  562.2 9.9 %copy.10 = bf16[1024,3584]{1,0:T(8,128)(2,1)} copy(bf16[1024,3584]{0,1:T(8,128)(2,1)} %all-reduce.3) | data formatting | bytes 14680064
  572.1 3.8 copy.12
  (8 shorter events, 0.1 us)
Async XLA Ops:
  7.2 5.8 copy-start
  7.2 218.8 %all-gather.2.cloned.1.call-start = ((), (), s32[]{:S(2)}) async-start(), calls=%async_computation.1 | async-start | bytes 5505024 | tf_op jit(solution)/shard_map/all_gather | solution.py:49
  11.2 561.0 %reduce-scatter.2.cloned.1.call-start = ((), (), s32[]{:S(2)}) async-start(), calls=%async_computation.2 | async-start | bytes 5505024 | tf_op jit(solution)/shard_map/reduce_scatter | solution.py:70
  19.5 14.8 %copy-start.1 = (f32[3584,512]{1,0:T(8,128)}, f32[3584,512]{1,0:T(8,128)S(1)}, u32[]{:S(2)}) copy-start(f32[3584,512]{1,0:T(8,128)S(1)} %fusion) | copy-start | bytes 22020100
Sparse Core Ops, SparseCore 0:
  11.3 18.0 all-gather.1
  226.0 8.0 reduce-scatter.1
where the time goes:
time: 583 us
  blocking collectives  498 us (85%)
  matrix products  36.3 us (6%)
  local copies, waits for them, and re-layouts  19.8 us (3%)
  other arithmetic  14.3 us (2%)
  between operations  14.1 us (2%)
    psum x1, blocking collectives, shards(): out_sum = lax.psum(out_part, 'col')  286 us
    psum x1, blocking collectives, total_squares(): return lax.psum(partial_squares, ('row', 'col'))  181 us
    psum x1, blocking collectives, shards(): back_sum = lax.psum(back_part, 'row')  31.6 us
    dot_general x2, matrix products, shards(): lax.dot_general(tokens, picked, (((0,), (0,)), ((), ())), preferred_eleme...  21.2 us
    unnamed x11, local copies, waits for them, and re-layouts  19.1 us
  transfers between devices with their start and end apart: 2, of which 0 were waited for; matrix products, arithmetic and copies ran while one was open for 11% of the time, Pallas kernels for 0%

commit v1 on v0

--- a/solution.py
+++ b/solution.py
@@ -54,8 +54,12 @@
     back_part = lax.dot_general(
         cotangent, masked_piece, (((1,), (1,)), ((), ())), preferred_element_type=jnp.float32
     )
-    out_sum = lax.psum(out_part, "col")
-    back_sum = lax.psum(back_part, "row")
+    out_sum = lax.all_gather(
+        lax.psum_scatter(out_part.astype(jnp.bfloat16), "col", scatter_dimension=0, tiled=True), "col", axis=0, tiled=True
+    )
+    back_sum = lax.all_gather(
+        lax.psum_scatter(back_part.astype(jnp.bfloat16), "row", scatter_dimension=0, tiled=True), "row", axis=0, tiled=True
+    )
     all_squares = total_squares(partial_squares)
     out_final = out_sum.astype(jnp.bfloat16)
     back_final = back_sum.astype(jnp.bfloat16)

time: 583 us -> 391 us (0.67)
  blocking collectives: 498 us -> 180 us
  waiting for transfers between devices: 0.06 us -> 117 us
  local copies, waits for them, and re-layouts: 19.8 us -> 31 us
    psum x2 -> x0, blocking collectives: 317 us -> none  [the longest x1 286 us: shards(): out_sum = lax.psum(out_part, 'col')]
    all_gather x0 -> x2, waiting for transfers between devices: none -> 91.4 us  [the longest x1 66.9 us: shards(): lax.all_gather(lax.psum_scatter(out_part.astype(jnp.bfloat16), 'col', sca...]
    all_gather x1, waiting for transfers between devices: 0.02 us -> 17.1 us  [shards(): lax.all_gather(weight, 'depth', axis=1, tiled=True)]
    unnamed x11 -> x18, local copies, waits for them, and re-layouts: 19.1 us -> 30.2 us
    reduce_scatter x1, waiting for transfers between devices: 0.01 us -> 7 us  [shards(): lax.psum_scatter(combined.astype(jnp.bfloat16), 'depth', scatter_dimensio...]
  transfers between devices with their start and end apart: 2 -> 6, of which waited for: 0 -> 4; matrix products, arithmetic and copies ran while one was open for 11% -> 15% of each run, Pallas kernels for 0% -> 0%
where the time goes in v1:
time: 391 us; the launch traced here: 390 us
  blocking collectives  180 us (46%)
  waiting for transfers between devices  117 us (30%)
  matrix products  33.9 us (9%)
  local copies, waits for them, and re-layouts  31 us (8%)
  between operations  14.2 us (4%)
  other arithmetic  14 us (4%)
    psum x1, blocking collectives, total_squares(): return lax.psum(partial_squares, ('row', 'col'))  180 us
    all_gather x1, waiting for transfers between devices, shards(): lax.all_gather(lax.psum_scatter(out_part.astype(jnp.bfloat16), 'col', sca...  66.9 us
    unnamed x18, local copies, waits for them, and re-layouts  30.2 us
    all_gather x1, waiting for transfers between devices, shards(): lax.all_gather(lax.psum_scatter(back_part.astype(jnp.bfloat16), 'row', sc...  24.5 us
    dot_general x2, matrix products, shards(): lax.dot_general(tokens, picked, (((0,), (0,)), ((), ())), preferred_eleme...  20.8 us
    all_gather x1, waiting for transfers between devices, shards(): lax.all_gather(weight, 'depth', axis=1, tiled=True)  17.1 us
    convert_element_type x1, other arithmetic, shards(): combined.astype(jnp.bfloat16)  9.33 us
    dot_general x1, matrix products, shards(): jnp.dot(tokens, jnp.where(kept, lax.all_gather(weight, 'depth', axis=1, t...  8.12 us
  transfers between devices with their start and end apart: 6, of which 4 were waited for; matrix products, arithmetic and copies ran while one was open for 15% of the time, Pallas kernels for 0%

profile of v1, /device:TPU:0, one launch (start us, length us, event | category | flops | bytes accessed | tf_op | source)
XLA Modules:
  0.0 389.8 jit_solution(2154121218663168929)
XLA Ops:
  7.2 3.9 %copy.14 = bf16[512,1792]{0,1:T(8,128)(2,1)} copy(bf16[512,1792]{1,0:T(8,128)(2,1)} %param.6) | data formatting | bytes 3670016 | tf_op args[1]
  11.2 0.8 dynamic-slice_compare_fusion.2
  12.3 17.1 %all-gather.4.cloned.1.call-done = bf16[512,3584]{0,1:T(8,128)(2,1)} async-done(((bf16[512,1792]{0,1:T(8,128)(2,1)}), bf16[512,3584]{0,1:T(8,128)(2,1)}) %all-gather.4.cloned.1.call-update) | async-done | bytes 3670032 | tf_op jit(solution)/shard_map/all_gather | solution.py:49
  29.4 2.5 bitcast_select_fusion.2
  31.9 1.9 copy-done.3
  33.7 1.2 copy-done.2
  34.9 5.0 %fusion.9 = bf16[1024,512]{0,1:T(8,128)(2,1)} fusion(bf16[512,3584]{0,1:T(8,128)(2,1)S(1)} %bitcast_select_fusion.2, bf16[1024,3584]{1,0:T(8,128)(2,1)S(1)} %copy-done.2), kind=kOutput, calls=%fused_computation.17 | convolution fusion | flops 3758620672 | bytes 12058624 | tf_op jit(solution)/shard_map/dot_general | solution.py:54
  40.0 8.1 %fusion.6 = bf16[1024,3584]{0,1:T(8,128)(2,1)} fusion(bf16[512,3584]{0,1:T(8,128)(2,1)} %copy-done.3, bf16[1024,512]{1,0:T(8,128)(2,1)S(1)} %copy-done), kind=kOutput, calls=%fused_computation.13 | convolution fusion | flops 3761766400 | bytes 12058624 | tf_op jit(solution)/shard_map/dot_general | solution.py:47
  48.1 10.0 %copy.18 = bf16[1024,3584]{1,0:T(8,128)(2,1)} copy(bf16[1024,3584]{0,1:T(8,128)(2,1)} %fusion.6) | data formatting | bytes 14680064
  58.4 0.4 copy-done.4
  58.8 6.5 %fusion = f32[3584,512]{1,0:T(8,128)S(1)} fusion(bf16[1024,512]{1,0:T(8,128)(2,1)S(1)} %copy-done, bf16[1024,3584]{1,0:T(8,128)(2,1)} %param.8, pred[1024]{0:T(1024)(128)(4,1)S(1)} %get-tuple-element.11), kind=kOutput, calls=%fused_computation.6 | convolution fusion | flops 3761766400 | bytes 15729664 | tf_op jit(solution)/shard_map/dot_general | solution.py:39
  65.4 14.3 %multiply_reduce_fusion.1 = (f32[]{:T(128)}, f32[]{:T(128)}, f32[3584,512]{1,0:T(8,128)}) fusion(pred[512,28]{0,1:T(8,128)(4,1)S(1)} %bitcast.46, f32[3584,512]{1,0:T(8,128)S(1)} %fusion, bf16[1024,512]{1,0:T(8,128)(2,1)S(1)} %copy-done, bf16[1024,3584]{1,0:T(8,128)(2,1)} %param.8, pred[1024]{0:T(1024)(128)(4,1)S(1)} %get-tuple-element.12), kind=kOutput, calls=%fused_computation.8 | convolution fusion | flops 3772776448 | bytes 23084040 | tf_op jit(solution)/shard_map/dot_general | solution.py:39
  79.6 1.4 pad_maximum_fusion
  81.0 179.6 %psum.7 = f32[2]{0:T(128)S(1)} all-reduce(f32[2]{0:T(128)S(1)} %pad_maximum_fusion), channel_id=1, replica_groups=mesh['row'=4,'col'=16,'depth'=2] {'row','col'}, use_global_device_ids=true, to_apply=%region_4.5 | all-reduce | flops 2 | bytes 16 | tf_op jit(solution)/shard_map/psum | solution.py:16
  260.7 0.7 fusion.12
  261.4 9.3 %multiply_convert_fusion = bf16[512,3584]{0,1:T(8,128)(2,1)} fusion(f32[3584,512]{1,0:T(8,128)} %get-tuple-element.15, f32[3584,512]{1,0:T(8,128)} %copy-done.1, f32[]{:T(128)} %bitcast.8, f32[]{:T(128)} %bitcast.7, pred[512,28]{0,1:T(8,128)(4,1)S(1)} %bitcast.47), kind=kLoop, calls=%fused_computation.4 | loop fusion | flops 12845056 | bytes 18364424 | tf_op jit(solution)/shard_map/convert_element_type | solution.py:75
  270.8 0.5 all-gather.8.cloned.1.call-update
  271.4 0.5 all-gather.6.cloned.1.call-update
  271.9 7.0 %reduce-scatter.8.cloned.1.call-done = bf16[512,1792]{0,1:T(8,128)(2,1)} async-done(((bf16[512,3584]{0,1:T(8,128)(2,1)}), bf16[512,1792]{0,1:T(8,128)(2,1)}) %reduce-scatter.8.cloned.1.call-update) | async-done | bytes 1835024 | tf_op jit(solution)/shard_map/reduce_scatter | solution.py:74
  278.9 3.8 copy.17
  282.7 24.5 %all-gather.8.cloned.1.call-done = bf16[1024,512]{0,1:T(8,128)(2,1)} async-done(((bf16[256,512]{0,1:T(8,128)(2,1)}), bf16[1024,512]{0,1:T(8,128)(2,1)}) %all-gather.8.cloned.1.call-update) | async-done | bytes 1048592 | tf_op jit(solution)/shard_map/all_gather | solution.py:60
  307.2 2.3 copy.16
  309.4 66.9 %all-gather.6.cloned.1.call-done = bf16[1024,3584]{1,0:T(8,128)(2,1)} async-done(((bf16[64,3584]{1,0:T(8,128)(2,1)}), bf16[1024,3584]{1,0:T(8,128)(2,1)}) %all-gather.6.cloned.1.call-update) | async-done | bytes 7340048 | tf_op jit(solution)/shard_map/all_gather | solution.py:57
  376.4 6.6 %copy.22 = bf16[1024,3584]{1,0:T(8,128)(2,1)} copy(bf16[1024,3584]{1,0:T(8,128)(2,1)} %all-gather.6.cloned.1.call-done) | data formatting | bytes 14680064
  (25 shorter events, 0.8 us)
Async XLA Ops:
  7.2 32.8 %copy-start = (bf16[1024,512]{1,0:T(8,128)(2,1)S(1)}, bf16[1024,512]{1,0:T(8,128)(2,1)}, u32[]{:S(2)}) copy-start(bf16[1024,512]{1,0:T(8,128)(2,1)} %param.5) | copy-start | bytes 3145732
  7.2 22.2 %all-gather.4.cloned.1.call-start = ((), (), s32[]{:S(2)}) async-start(), calls=%async_computation.3 | async-start | bytes 5505024 | tf_op jit(solution)/shard_map/all_gather | solution.py:49
  11.2 259.6 %reduce-scatter.6.cloned.1.call-start = ((), (), s32[]{:S(2)}) async-start(), calls=%async_computation.5 | async-start | bytes 1310720 | tf_op jit(solution)/shard_map/reduce_scatter | solution.py:61
  29.4 5.5 %copy-start.2 = (bf16[1024,3584]{1,0:T(8,128)(2,1)S(1)}, bf16[1024,3584]{1,0:T(8,128)(2,1)}, u32[]{:S(2)}) copy-start(bf16[1024,3584]{1,0:T(8,128)(2,1)} %param.8) | copy-start | bytes 22020100
  31.9 1.9 copy-start.3
  39.9 231.5 %reduce-scatter.10.cloned.1.call-start = ((), (), s32[]{:S(2)}) async-start(), calls=%async_computation.8 | async-start | bytes 7798784 | tf_op jit(solution)/shard_map/reduce_scatter | solution.py:58
  58.1 0.7 copy-start.4
  58.1 220.7 %reduce-scatter.8.cloned.1.call-start = ((), (), s32[]{:S(2)}) async-start(), calls=%async_computation.7 | async-start | bytes 5505024 | tf_op jit(solution)/shard_map/reduce_scatter | solution.py:74
  65.4 14.3 %copy-start.1 = (f32[3584,512]{1,0:T(8,128)}, f32[3584,512]{1,0:T(8,128)S(1)}, u32[]{:S(2)}) copy-start(f32[3584,512]{1,0:T(8,128)S(1)} %fusion) | copy-start | bytes 22020100
  270.7 36.4 %all-gather.8.cloned.1.call-start = ((), (), s32[]{:S(2)}) async-start(), calls=%async_computation.6 | async-start | bytes 1310720 | tf_op jit(solution)/shard_map/all_gather | solution.py:60
  271.3 105.1 %all-gather.6.cloned.1.call-start = ((), (), s32[]{:S(2)}) async-start(), calls=%async_computation.4 | async-start | bytes 7798784 | tf_op jit(solution)/shard_map/all_gather | solution.py:57
Sparse Core Ops, SparseCore 0:
  11.3 18.0 all-gather.3
  40.0 24.9 reduce-scatter.5
  68.5 83.6 reduce-scatter.9
  270.8 8.0 reduce-scatter.7
  280.4 26.7 all-gather.7
  309.1 67.1 all-gather.5

commit v2 on v0

v2 whole, which is shorter than its diff:
```python
import math

import jax
import jax.numpy as jnp
from jax import lax
from jax.experimental import pallas as pl
from jax.experimental.pallas import tpu as pltpu
from jax.sharding import PartitionSpec as P

D = 8192
FW = 14336
BLOCK = 128
TOK_DEV = 1024
EX_DEV = 2
RING = 4
TILE = 256

MESH = pl.DeviceIdType.MESH
F32 = jnp.float32
BF16 = jnp.bfloat16


def kernel(
    tok_ref, w_ref, g_ref, keep_ref, pick_ref,
    out_ref, back_ref, gw_ref,
    x, xt, w, g, part, red, fin,
    fwd1, rcv1, fwd2, rcv2,
    prod, sq, bpart, brcv, bsum, blk, brecv, nrm, nrcv,
    send_sem, recv_sem, local_sem,
):
    row, col, dep = lax.axis_index("row"), lax.axis_index("col"), lax.axis_index("depth")
    y, z = lax.rem(col, RING), lax.div(col, RING)
    other = 1 - dep
    tok_rows, width = x.shape
    half = w.shape[2]
    lane_half = half // 2
    tiles = half // TILE
    crow = tok_rows // 2
    q1 = crow // RING
    q2 = q1 // RING
    qx = tok_rows // RING

    def turn(at, k):
        return lax.rem(at + (k + RING), RING)

    def device(axis, k):
        if axis == "x":
            return (turn(row, k), col, dep)
        if axis == "y":
            return (row, z * RING + turn(y, k), dep)
        if axis == "z":
            return (row, turn(z, k) * RING + y, dep)
        return (row, col, other)

    place = {"x": row, "y": y, "z": z}
    started = []
    local_started = []

    def remote(src, dst, to):
        k = len(started)
        copy = pltpu.make_async_remote_copy(
            src_ref=src, dst_ref=dst, send_sem=send_sem.at[k], recv_sem=recv_sem.at[k],
            device_id=to, device_id_type=MESH,
        )
        copy.start()
        started.append(copy)
        return copy

    def local(src, dst):
        copy = pltpu.make_async_copy(src, dst, local_sem.at[len(local_started)])
        copy.start()
        local_started.append(copy)
        return copy

    load_x = local(tok_ref, x)
    load_w = local(w_ref, w.at[dep])
    load_g = [local(g_ref.at[:, pl.ds(h * half, half)], g.at[h]) for h in range(2)]
    peers = [device(axis, k) for axis in ("y", "z", "x") for k in (1, 2, 3)] + [device("d", 1)]
    barrier = pltpu.get_barrier_semaphore()
    for peer in peers:
        pl.semaphore_signal(barrier, inc=1, device_id=peer, device_id_type=MESH)
    pl.semaphore_wait(barrier, len(peers))

    swap_w = remote(w_ref, w.at[dep], device("d", 1))

    left, right = pl.ds(0, lane_half), pl.ds(lane_half, lane_half)

    def add_into(size, dst, terms):
        def step(i, c):
            at = pl.ds(pl.multiple_of(i * 16, 16), 16)
            total = terms[0][at, :].astype(F32)
            for term in terms[1:]:
                total = total + term[at, :].astype(F32)
            dst[at, :] = total.astype(BF16)
            return c
        lax.fori_loop(0, size // 16, step, 0)

    class Reduce:
        def __init__(self, axis, size, src, fwd, rcv, dst):
            self.axis, self.size, self.fwd, self.rcv, self.dst = axis, size, fwd, rcv, dst
            me = place[axis]
            self.piece = lambda k: src.at[pl.ds(pl.multiple_of(turn(me, k) * size, size), size), :]
            self.up, self.down = device(axis, 1), device(axis, -1)

        def start(self):
            far, near, back = self.piece(2), self.piece(1), self.piece(-1)
            self.a = [
                remote(far.at[:, left], self.fwd.at[0], self.up),
                remote(far.at[:, right], self.fwd.at[1], self.down),
            ]
            self.b = [
                remote(near.at[:, right], self.rcv.at[0, :, right], self.up),
                remote(back.at[:, left], self.rcv.at[1, :, left], self.down),
            ]

        def mid(self):
            near, back = self.piece(1).at[:, left], self.piece(-1).at[:, right]
            self.a[0].wait_recv()
            add_into(self.size, near, [near, self.fwd.at[0]])
            c0 = remote(near, self.rcv.at[0, :, left], self.up)
            self.a[1].wait_recv()
            add_into(self.size, back, [back, self.fwd.at[1]])
            c1 = remote(back, self.rcv.at[1, :, right], self.down)
            self.c = [c0, c1]

        def end(self):
            for copy in self.b + self.c:
                copy.wait_recv()
            add_into(self.size, self.dst, [self.piece(0), self.rcv.at[0], self.rcv.at[1]])

    class Gather:
        def __init__(self, axis, dst):
            self.dst, me = dst, place[axis]
            self.at = lambda k: dst(turn(me, k))
            self.up, self.down = device(axis, 1), device(axis, -1)

        def start(self, src):
            own = self.at(0)
            self.ul = remote(src.at[:, left], own.at[:, left], self.up)
            self.dr = remote(src.at[:, right], own.at[:, right], self.down)
            self.ur = remote(src.at[:, right], own.at[:, right], self.up)
            self.dl = remote(src.at[:, left], own.at[:, left], self.down)

        def mid(self):
            below, above = self.at(-1).at[:, left], self.at(1).at[:, right]
            self.ul.wait_recv()
            self.f0 = remote(below, below, self.up)
            self.dr.wait_recv()
            self.f1 = remote(above, above, self.down)

        def end(self):
            for copy in (self.ur, self.dl, self.f0, self.f1):
                copy.wait_recv()

    subs = []
    for s in range(4):
        first, second = ("y", "z") if s % 2 == 0 else ("z", "y")
        base = (s % 2) * crow
        cols = pl.ds(pl.multiple_of((dep if s < 2 else other) * half, BLOCK), half)
        i1, i2 = place[first], place[second]

        def inner(i, base=base, cols=cols, i1=i1):
            return out_ref.at[pl.ds(pl.multiple_of(base + i1 * q1 + i * q2, q2), q2), cols]

        def outer(i, base=base, cols=cols):
            return out_ref.at[pl.ds(pl.multiple_of(base + i * q1, q1), q1), cols]

        subs.append(dict(
            r1=Reduce(first, q1, part.at[s], fwd1.at[s], rcv1.at[s], red.at[s]),
            r2=Reduce(second, q2, red.at[s], fwd2.at[s], rcv2.at[s], fin.at[s]),
            a1=Gather(second, inner), a2=Gather(first, outer), fin=fin.at[s],
        ))

    def r1_end(s):
        subs[s]["r1"].end()
        subs[s]["r2"].start()

    def r2_mid(s):
        subs[s]["r2"].mid()

    def r2_end(s):
        subs[s]["r2"].end()
        sub = subs[s]
        sub["a1"].start(sub["fin"])
        sub["own"] = local(sub["fin"], sub["a1"].at(0))

    def a1_mid(s):
        subs[s]["a1"].mid()

    def a1_end(s):
        sub = subs[s]
        sub["a1"].end()
        sub["own"].wait()
        sub["a2"].start(sub["a2"].at(0))

    def a2_mid(s):
        subs[s]["a2"].mid()

    def a2_end(s):
        subs[s]["a2"].end()

    def part_dot(s, mask):
        h = dep if s < 2 else other
        rows = pl.ds((s % 2) * crow, crow)

        def step(j, c):
            at = pl.ds(pl.multiple_of(j * TILE, TILE), TILE)
            if mask:
                for kb in range(width // BLOCK):
                    ks = pl.ds(kb * BLOCK, BLOCK)
                    kept = keep_ref[h, kb:kb + 1, at] > 0
                    w[h, ks, at] = jnp.where(kept, w[h, ks, at].astype(F32), 0.0).astype(BF16)
            part[s, :, at] = jnp.dot(x[rows, :], w[h, :, at], preferred_element_type=F32).astype(BF16)
            return c

        lax.fori_loop(0, tiles, step, 0)

    def make_xt():
        for i in range(tok_rows // TILE):
            at = pl.ds(i * TILE, TILE)
            flipped = jnp.transpose(x[at, :].astype(F32))
            for slot in range(EX_DEV):
                chosen = pick_ref[slot:slot + 1, at] > 0
                xt[slot, :, at] = jnp.where(chosen, flipped, 0.0).astype(BF16)

    def products(h, first, last):
        def step(j, c):
            at = pl.ds(pl.multiple_of(j * TILE, TILE), TILE)
            for slot in range(EX_DEV):
                value = jnp.dot(xt[slot], g[h, :, at], preferred_element_type=F32)
                total = sq[slot]
                for kb in range(width // BLOCK):
                    kept = keep_ref[h, kb:kb + 1, at] > 0
                    piece = jnp.where(kept, value[kb * BLOCK:(kb + 1) * BLOCK, :], 0.0)
                    prod[slot, h, pl.ds(kb * BLOCK, BLOCK), at] = piece
                    total = total + jnp.sum((piece * piece).reshape(BLOCK // 8, 8, TILE), axis=0)
                sq[slot] = total
            return c

        lax.fori_loop(first, last, step, 0)

    def back_dot():
        def step(i, c):
            rows = pl.ds(pl.multiple_of(i * TILE, TILE), TILE)
            total = None
            for h in range(2):
                term = lax.dot_general(
                    g[h, rows, :], w[h], (((1,), (1,)), ((), ())), preferred_element_type=F32
                )
                total = term if total is None else total + term
            bpart[rows, :] = total.astype(BF16)
            return c

        lax.fori_loop(0, tok_rows // TILE, step, 0)

    quarter = lambda ref, i: ref.at[pl.ds(pl.multiple_of(i * qx, qx), qx), :]
    state = {}

    def back_send():
        state["b"] = [remote(quarter(bpart, turn(row, k)), brcv.at[k - 1], device("x", k)) for k in (2, 1, 3)]

    def back_sum():
        for copy in state["b"]:
            copy.wait_recv()
        add_into(qx, bsum, [quarter(bpart, row), brcv.at[0], brcv.at[1], brcv.at[2]])
        state["bg"] = [remote(bsum, quarter(back_ref, row), device("x", k)) for k in (2, 1, 3)]
        state["bl"] = local(bsum, quarter(back_ref, row))

    def norm_first():
        rows = lax.broadcasted_iota(jnp.int32, (8, TILE), 0)
        first, second = jnp.sum(sq[0]), jnp.sum(sq[1])
        nrm[0] = jnp.where(rows == 0, first, jnp.where(rows == 1, second, 0.0))

    def norm_send(stage):
        axis = "xyz"[stage]
        state["n"] = [remote(nrm.at[stage], nrcv.at[stage, k - 1], device(axis, k)) for k in (1, 2, 3)]

    def norm_sum(stage):
        for copy in state["n"]:
            copy.wait_recv()
        nrm[stage + 1] = nrm[stage] + nrcv[stage, 0] + nrcv[stage, 1] + nrcv[stage, 2]

    def block_sums():
        bound = F32(0.5 * math.sqrt(D * FW * TOK_DEV))
        factors = bound / jnp.maximum(jnp.sqrt(nrm[3]), bound)
        f0, f1 = factors[0:1, :], factors[1:2, :]

        for h in range(2):
            def step(j, c, h=h):
                at = pl.ds(pl.multiple_of(j * TILE, TILE), TILE)
                total = f0 * prod[0, h, :, at] + f1 * prod[1, h, :, at]
                blk[h, :, at] = (total * 0.25).astype(BF16)
                return c
            lax.fori_loop(0, tiles, step, 0)
        state["w"] = remote(blk.at[other], brecv, device("d", 1))

    def weight_sum():
        state["w"].wait_recv()
        add_into(width, brecv, [blk.at[dep], brecv])
        state["wl"] = local(brecv, gw_ref)

    load_x.wait()
    load_w.wait()
    part_dot(0, True)
    subs[0]["r1"].start()
    part_dot(1, False)
    subs[1]["r1"].start()
    swap_w.wait_recv()
    part_dot(2, True)
    part_dot(3, False)
    subs[0]["r1"].mid()
    subs[2]["r1"].start()
    subs[1]["r1"].mid()
    subs[3]["r1"].start()
    make_xt()
    for slot in range(EX_DEV):
        sq[slot] = jnp.zeros((8, TILE), F32)
    for copy in load_g:
        copy.wait()
    products(0, 0, 5)
    r1_end(0)
    r1_end(1)
    products(0, 5, tiles)
    products(1, 0, 3)
    subs[2]["r1"].mid()
    subs[3]["r1"].mid()
    r2_mid(0)
    r2_mid(1)
    products(1, 3, tiles)
    norm_first()
    norm_send(0)
    r2_end(0)
    r2_end(1)
    back_dot()
    back_send()
    norm_sum(0)
    norm_send(1)
    a1_mid(0)
    a1_mid(1)
    r1_end(2)
    r1_end(3)
    a1_end(0)
    a1_end(1)
    norm_sum(1)
    norm_send(2)
    r2_mid(2)
    r2_mid(3)
    back_sum()
    norm_sum(2)
    block_sums()
    r2_end(2)
    r2_end(3)
    a2_mid(0)
    a2_mid(1)
    a1_mid(2)
    a1_mid(3)
    weight_sum()
    a1_end(2)
    a1_end(3)
    a2_end(0)
    a2_end(1)
    a2_mid(2)
    a2_mid(3)
    for copy in state["bg"]:
        copy.wait_recv()
    a2_end(2)
    a2_end(3)
    for copy in started:
        copy.wait_send()
    state["bl"].wait()
    state["wl"].wait()


def shards(tokens, weight, block_mask, cotangent, example_ids):
    tok_rows, width = tokens.shape
    half = weight.shape[1]
    hidden = cotangent.shape[1]
    col_at, row_at, depth_at = lax.axis_index("col"), lax.axis_index("row"), lax.axis_index("depth")
    deep, wide = width // BLOCK, hidden // BLOCK
    tile_mask = lax.dynamic_slice(block_mask, (col_at * deep, row_at * wide), (deep, wide))
    keep = jnp.repeat((tile_mask > 0).astype(F32), BLOCK, axis=1).reshape(deep, 2, half).transpose(1, 0, 2)
    ids_here = lax.dynamic_slice_in_dim(example_ids, depth_at * tok_rows, tok_rows)
    pick = (ids_here[None, :] == depth_at * EX_DEV + jnp.arange(EX_DEV, dtype=jnp.int32)[:, None]).astype(F32)
    crow = tok_rows // 2
    q1, q2, qx = crow // RING, crow // RING // RING, tok_rows // RING
    vmem = pl.BlockSpec(memory_space=pltpu.VMEM)
    anywhere = pl.BlockSpec(memory_space=pl.ANY)
    copies = 1 + 4 * 24 + 6 + 9 + 1
    return pl.pallas_call(
        kernel,
        out_shape=(
            jax.ShapeDtypeStruct((tok_rows, hidden), BF16),
            jax.ShapeDtypeStruct((tok_rows, width), BF16),
            jax.ShapeDtypeStruct((width, half), BF16),
        ),
        in_specs=[anywhere, anywhere, anywhere, vmem, vmem],
        out_specs=(anywhere, anywhere, anywhere),
        scratch_shapes=[
            pltpu.VMEM((tok_rows, width), BF16),
            pltpu.VMEM((EX_DEV, width, tok_rows), BF16),
            pltpu.VMEM((2, width, half), BF16),
            pltpu.VMEM((2, tok_rows, half), BF16),
            pltpu.VMEM((4, crow, half), BF16),
            pltpu.VMEM((4, q1, half), BF16),
            pltpu.VMEM((4, q2, half), BF16),
            pltpu.VMEM((4, 2, q1, half // 2), BF16),
            pltpu.VMEM((4, 2, q1, half), BF16),
            pltpu.VMEM((4, 2, q2, half // 2), BF16),
            pltpu.VMEM((4, 2, q2, half), BF16),
            pltpu.VMEM((EX_DEV, 2, width, half), F32),
            pltpu.VMEM((EX_DEV, 8, TILE), F32),
            pltpu.VMEM((tok_rows, width), BF16),
            pltpu.VMEM((3, qx, width), BF16),
            pltpu.VMEM((qx, width), BF16),
            pltpu.VMEM((2, width, half), BF16),
            pltpu.VMEM((width, half), BF16),
            pltpu.VMEM((4, 8, TILE), F32),
            pltpu.VMEM((3, 3, 8, TILE), F32),
            pltpu.SemaphoreType.DMA((copies,)),
            pltpu.SemaphoreType.DMA((copies,)),
            pltpu.SemaphoreType.DMA((10,)),
        ],
        compiler_params=pltpu.CompilerParams(
            collective_id=0, has_side_effects=True, vmem_limit_bytes=67_000_000
        ),
        name="whole_layer",
    )(tokens, weight, cotangent, keep, pick)


def solution(mesh):
    placed = (P("depth", "col"), P("col", ("row", "depth")), P(), P("depth", "row"), P())
    return jax.shard_map(
        shards,
        mesh=mesh,
        in_specs=placed,
        out_specs=(P("depth", "row"), P("depth", "col"), P("col", ("row", "depth"))),
        check_vma=False,
    )
```

time: 583 us -> 108 us (0.19)
  blocking collectives: 498 us -> 0 us
  Pallas kernels: 0 us -> 95.2 us
  matrix products: 36.3 us -> 0 us
  between operations: 14.1 us -> 0.68 us
  other arithmetic: 14.3 us -> 1.44 us
  local copies, waits for them, and re-layouts: 19.8 us -> 10.4 us
    psum x3 -> x0, blocking collectives: 498 us -> none  [the longest x1 286 us: shards(): out_sum = lax.psum(out_part, 'col')]
    pallas_call x0 -> x1, Pallas kernels: none -> 95.2 us  [shards(): pl.pallas_call(kernel, out_shape=(jax.ShapeDtypeStruct((tok_rows, hidden)...]
    dot_general x4 -> x0, matrix products: 36.3 us -> none  [the longest x2 21.2 us: shards(): lax.dot_general(tokens, picked, (((0,), (0,)), ((), ())), preferred_eleme...]
    unnamed x11 -> x7, local copies, waits for them, and re-layouts: 19.1 us -> 8.96 us
    convert_element_type x1 -> x2, other arithmetic: 9.23 us -> 1.44 us  [the longest x1 0.77 us: shards(): (tile_mask > 0).astype(F32)]
  transfers between devices with their start and end apart: 2 -> 0, of which waited for: 0 -> 0; matrix products, arithmetic and copies ran while one was open for 11% -> 0% of each run, Pallas kernels for 0% -> 0%
where the time goes in v2:
time: 108 us
  Pallas kernels  95.2 us (88%)
  local copies, waits for them, and re-layouts  10.4 us (10%)
  other arithmetic  1.44 us (1%)
    pallas_call x1, Pallas kernels, shards(): pl.pallas_call(kernel, out_shape=(jax.ShapeDtypeStruct((tok_rows, hidden)...  95.2 us
    unnamed x7, local copies, waits for them, and re-layouts  8.96 us

profile of v2, /device:TPU:0, one launch (start us, length us, event | category | flops | bytes accessed | tf_op | source)
XLA Modules:
  0.0 107.8 jit_solution(17042160041651143)
XLA Ops:
  0.6 0.8 fusion
  1.4 0.7 dynamic_slice.7
  2.1 0.7 compare_convert_fusion.pick_ref
  2.8 0.1 broadcast_in_dim.2
  2.9 0.6 copy.10
  3.5 95.2 %whole_layer.1 = (bf16[1024,3584]{1,0:T(8,128)(2,1)}, bf16[1024,512]{1,0:T(8,128)(2,1)}, bf16[512,1792]{1,0:T(8,128)(2,1)}) custom-call(bf16[1024,512]{1,0:T(8,128)(2,1)} %tok_ref.1, bf16[512,1792]{1,0:T(8,128)(2,1)} %w_ref.1, bf16[1024,3584]{1,0:T(8,128)(2,1)} %g_ref.1, f32[2,4,1792]{2,1,0:T(4,128)} %bitcast.3, f32[2,1024]{1,0:T(2,128)} %compare_convert_fusion.pick_ref), custom_call_target="tpu_custom_call" | custom-call | tf_op jit(solution)/shard_map/whole_layer/pallas_call | solution.py:389
  98.8 0.0 copy-start.1
  98.8 0.0 copy-start
  98.8 6.8 %copy.14 = bf16[1024,3584]{1,0:T(8,128)(2,1)} copy(bf16[1024,3584]{1,0:T(8,128)(2,1)} %get-tuple-element.6) | data formatting | bytes 14680064
  105.6 0.0 copy-done.1
  105.6 1.0 copy.15
  106.5 0.0 copy-done
  106.5 1.2 %copy.16 = bf16[512,1792]{1,0:T(8,128)(2,1)} copy(bf16[512,1792]{1,0:T(8,128)(2,1)S(1)} %copy-done) | data formatting | bytes 3670016
  (2 shorter events, 0.0 us)
Async XLA Ops:
  98.8 6.8 %copy-start.1 = (bf16[1024,512]{1,0:T(8,128)(2,1)S(1)}, bf16[1024,512]{1,0:T(8,128)(2,1)}, u32[]{:S(2)}) copy-start(bf16[1024,512]{1,0:T(8,128)(2,1)} %get-tuple-element.7) | copy-start | bytes 3145732
  98.8 7.7 %copy-start = (bf16[512,1792]{1,0:T(8,128)(2,1)S(1)}, bf16[512,1792]{1,0:T(8,128)(2,1)}, u32[]{:S(2)}) copy-start(bf16[512,1792]{1,0:T(8,128)(2,1)} %get-tuple-element.8) | copy-start | bytes 5505028

commit v3 on v2

--- a/solution.py
+++ b/solution.py
@@ -21,11 +21,11 @@
 
 
 def kernel(
-    tok_ref, w_ref, g_ref, keep_ref, pick_ref,
+    tok_ref, w_ref, g_ref, mask_ref, ids_ref,
     out_ref, back_ref, gw_ref,
     x, xt, w, g, part, red, fin,
     fwd1, rcv1, fwd2, rcv2,
-    prod, sq, bpart, brcv, bsum, blk, brecv, nrm, nrcv,
+    prod, sq, bpart, brcv, bsum, blk, brecv, nrm, nrcv, keep_ref,
     send_sem, recv_sem, local_sem,
 ):
     row, col, dep = lax.axis_index("row"), lax.axis_index("col"), lax.axis_index("depth")
@@ -79,10 +79,6 @@
     barrier = pltpu.get_barrier_semaphore()
     for peer in peers:
         pl.semaphore_signal(barrier, inc=1, device_id=peer, device_id_type=MESH)
-    pl.semaphore_wait(barrier, len(peers))
-
-    swap_w = remote(w_ref, w.at[dep], device("d", 1))
-
     left, right = pl.ds(0, lane_half), pl.ds(lane_half, lane_half)
 
     def add_into(size, dst, terms):
@@ -199,6 +195,20 @@
     def a2_end(s):
         subs[s]["a2"].end()
 
+    def expand_mask():
+        blocks_in, blocks_out = mask_ref.shape
+        deep, wide = width // BLOCK, 2 * half // BLOCK
+        kept = (mask_ref[...] > 0).astype(F32).astype(BF16)
+        here = lax.broadcasted_iota(jnp.int32, (8, blocks_in), 0)
+        there = lax.broadcasted_iota(jnp.int32, (8, blocks_in), 1)
+        pick_rows = ((there == here + col * deep) & (here < deep)).astype(F32).astype(BF16)
+        rows = jnp.dot(pick_rows, kept, preferred_element_type=F32).astype(BF16)
+        block = lax.broadcasted_iota(jnp.int32, (blocks_out, half), 0)
+        lane = lax.broadcasted_iota(jnp.int32, (blocks_out, half), 1)
+        for h in range(2):
+            spread = (block == row * wide + h * (half // BLOCK) + lane // BLOCK).astype(F32).astype(BF16)
+            keep_ref[h] = jnp.dot(rows, spread, preferred_element_type=F32)
+
     def part_dot(s, mask):
         h = dep if s < 2 else other
         rows = pl.ds((s % 2) * crow, crow)
@@ -216,11 +226,14 @@
         lax.fori_loop(0, tiles, step, 0)
 
     def make_xt():
+        first_id = (ids_ref[...] == dep * EX_DEV).astype(F32)
+        run = jnp.sum(jnp.sum(first_id, axis=0, keepdims=True), axis=1, keepdims=True)
+        token = lax.broadcasted_iota(jnp.int32, (1, TILE), 1).astype(F32)
         for i in range(tok_rows // TILE):
             at = pl.ds(i * TILE, TILE)
             flipped = jnp.transpose(x[at, :].astype(F32))
             for slot in range(EX_DEV):
-                chosen = pick_ref[slot:slot + 1, at] > 0
+                chosen = (token + i * TILE < run) if slot == 0 else (token + i * TILE >= run)
                 xt[slot, :, at] = jnp.where(chosen, flipped, 0.0).astype(BF16)
 
     def products(h, first, last):
@@ -299,9 +312,12 @@
         add_into(width, brecv, [blk.at[dep], brecv])
         state["wl"] = local(brecv, gw_ref)
 
+    expand_mask()
     load_x.wait()
     load_w.wait()
     part_dot(0, True)
+    pl.semaphore_wait(barrier, len(peers))
+    swap_w = remote(w_ref, w.at[dep], device("d", 1))
     subs[0]["r1"].start()
     part_dot(1, False)
     subs[1]["r1"].start()
@@ -375,12 +391,7 @@
     tok_rows, width = tokens.shape
     half = weight.shape[1]
     hidden = cotangent.shape[1]
-    col_at, row_at, depth_at = lax.axis_index("col"), lax.axis_index("row"), lax.axis_index("depth")
-    deep, wide = width // BLOCK, hidden // BLOCK
-    tile_mask = lax.dynamic_slice(block_mask, (col_at * deep, row_at * wide), (deep, wide))
-    keep = jnp.repeat((tile_mask > 0).astype(F32), BLOCK, axis=1).reshape(deep, 2, half).transpose(1, 0, 2)
-    ids_here = lax.dynamic_slice_in_dim(example_ids, depth_at * tok_rows, tok_rows)
-    pick = (ids_here[None, :] == depth_at * EX_DEV + jnp.arange(EX_DEV, dtype=jnp.int32)[:, None]).astype(F32)
+    ids = example_ids.reshape(-1, BLOCK)
     crow = tok_rows // 2
     q1, q2, qx = crow // RING, crow // RING // RING, tok_rows // RING
     vmem = pl.BlockSpec(memory_space=pltpu.VMEM)
@@ -389,12 +400,12 @@
     return pl.pallas_call(
         kernel,
         out_shape=(
-            jax.ShapeDtypeStruct((tok_rows, hidden), BF16),
-            jax.ShapeDtypeStruct((tok_rows, width), BF16),
-            jax.ShapeDtypeStruct((width, half), BF16),
+            pltpu.VMEM((tok_rows, hidden), BF16),
+            pltpu.VMEM((tok_rows, width), BF16),
+            pltpu.VMEM((width, half), BF16),
         ),
         in_specs=[anywhere, anywhere, anywhere, vmem, vmem],
-        out_specs=(anywhere, anywhere, anywhere),
+        out_specs=(vmem, vmem, vmem),
         scratch_shapes=[
             pltpu.VMEM((tok_rows, width), BF16),
             pltpu.VMEM((EX_DEV, width, tok_rows), BF16),
@@ -416,15 +427,16 @@
             pltpu.VMEM((width, half), BF16),
             pltpu.VMEM((4, 8, TILE), F32),
             pltpu.VMEM((3, 3, 8, TILE), F32),
+            pltpu.VMEM((2, 8, half), F32),
             pltpu.SemaphoreType.DMA((copies,)),
             pltpu.SemaphoreType.DMA((copies,)),
             pltpu.SemaphoreType.DMA((10,)),
         ],
         compiler_params=pltpu.CompilerParams(
-            collective_id=0, has_side_effects=True, vmem_limit_bytes=67_000_000
+            collective_id=0, has_side_effects=True, vmem_limit_bytes=56_000_000
         ),
         name="whole_layer",
-    )(tokens, weight, cotangent, keep, pick)
+    )(tokens, weight, cotangent, block_mask, ids)
 
 
 def solution(mesh):

time: 108 us -> 101 us (0.935)
  local copies, waits for them, and re-layouts: 10.4 us -> 5.25 us
  other arithmetic: 1.44 us -> 0 us
    unnamed x7 -> x3, local copies, waits for them, and re-layouts: 8.96 us -> 5.25 us
    convert_element_type x2 -> x0, other arithmetic: 1.44 us -> none  [the longest x1 0.77 us: shards(): (tile_mask > 0).astype(F32)]
where the time goes in v3:
time: 101 us
  Pallas kernels  94.9 us (94%)
  local copies, waits for them, and re-layouts  5.25 us (5%)
    pallas_call x1, Pallas kernels, shards(): pl.pallas_call(kernel, out_shape=(pltpu.VMEM((tok_rows, hidden), BF16), p...  94.9 us
    unnamed x3, local copies, waits for them, and re-layouts  5.25 us

profile of v3, /device:TPU:0, one launch (start us, length us, event | category | flops | bytes accessed | tf_op | source)
XLA Modules:
  0.0 100.8 jit_solution(15987983440986750164)
XLA Ops:
  0.6 94.9 %whole_layer.1 = (bf16[1024,3584]{1,0:T(8,128)(2,1)S(1)}, bf16[1024,512]{1,0:T(8,128)(2,1)S(1)}, bf16[512,1792]{1,0:T(8,128)(2,1)S(1)}) custom-call(bf16[1024,512]{1,0:T(8,128)(2,1)} %tok_ref.1, bf16[512,1792]{1,0:T(8,128)(2,1)} %w_ref.1, bf16[1024,3584]{1,0:T(8,128)(2,1)} %g_ref.1, s32[64,112]{1,0:T(8,128)} %mask_ref.1, s32[16,128]{1,0:T(8,128)} %bitcast.1), custom_call_target="tpu_custom_call" | custom-call | tf_op jit(solution)/shard_map/whole_layer/pallas_call | solution.py:400
  95.5 3.1 %copy.11 = bf16[1024,3584]{1,0:T(8,128)(2,1)} copy(bf16[1024,3584]{1,0:T(8,128)(2,1)S(1)} %get-tuple-element.3) | data formatting | bytes 14680064
  98.6 1.0 copy.12
  99.6 1.2 %copy.13 = bf16[512,1792]{1,0:T(8,128)(2,1)} copy(bf16[512,1792]{1,0:T(8,128)(2,1)S(1)} %get-tuple-element.5) | data formatting | bytes 3670016
